TPU v7x, 32 devices: a whole 2x2x4 slice. The times are simulated.
32 devices in a mesh: tile: 8 (over y, x, core), sec: 4 (over z).
Axes of the slice: x: 2, y: 2, z: 4, core: 2. Of those that a mesh axis runs over, the one named last changes fastest.
Arguments:
- pixels: bfloat16 [8, 64, 1024, 256], P('sec', 'tile'), may hold values from -6 to 6
- pred_features: bfloat16 [64, 1024, 128], P('tile'), may hold values from -6 to 6
- offsets: int32 [8, 2, 64, 1024], P('sec', None, 'tile'), may hold values from -1 to 1
- valid_mask: int32 [8, 64, 1024], P('sec', 'tile'), may hold values 0 or 1
- base_shift: float32 [2, 64, 1024], P(None, 'tile'), may hold values from -6 to 6
- w_hidden: bfloat16 [256, 512], replicated, may hold values from -0.375 to 0.375
- w_feature: bfloat16 [512, 128], replicated, may hold values from -0.25 to 0.25
- feat_gain: float32 [128], replicated, may hold values from 0.25 to 1.75
Outputs:
- displacement: float32 [8, 2, 64, 1024], P('sec', None, 'tile')
All inputs are finite; a program needn't handle non-finite values. No bound on the sum of `valid_mask` on one device may be relied on, other than what follows from the above.
Results may differ from a plain program's by a relative error of at most 0.0024.
Values may be sent and summed in bfloat16 or wider, within the bound.
No kernel may reach another device: no remote copies, remote signals or barrier semaphores. Data moves between devices by JAX's collectives and lax.ppermute only.
A program may use at most 128 MiB of HBM per device.

v0:
```python
import jax
import jax.numpy as jnp
from jax import lax
from jax.sharding import PartitionSpec as P

ITERS = 8


epsilon = 1e-05
step_size = 0.2
stiffness = 0.5


def from_behind(value, axis, steps):
    count = lax.axis_size(axis)
    first, last = (max(0, -steps), min(count, count - steps))
    return lax.ppermute(value, axis, [(source, source + steps) for source in range(first, last)])


def with_halo(cells, sides, width):
    for axis, dim in sides:
        count = lax.axis_size(axis)
        ends = count - 1
        head = lax.slice_in_dim(cells, 0, width, axis=dim)
        tail = lax.slice_in_dim(cells, cells.shape[dim] - width, cells.shape[dim], axis=dim)
        cells = jnp.concatenate(
            [
                lax.ppermute(tail, axis, [(i, (i + 1) % count) for i in range(ends)]),
                cells,
                lax.ppermute(head, axis, [((i + 1) % count, i) for i in range(ends)]),
            ],
            axis=dim,
        )
    return cells


def entering(value, axis, join, neutral):
    place = lax.axis_index(axis)
    gathered = lax.all_gather(
        value.astype(jnp.bfloat16 if value.dtype == jnp.float32 else value.dtype), axis
    )
    state = jnp.zeros_like(value) + jnp.asarray(neutral, value.dtype)

    def one(hop, state):
        return join(state, lax.dynamic_index_in_dim(gathered, hop, 0, False).astype(value.dtype))

    return lax.fori_loop(0, place, one, state)


def encode(section_pixels, w_hidden, w_feature, feat_gain):
    flat = section_pixels.reshape(-1, section_pixels.shape[-1])
    hidden = jax.nn.relu(jnp.dot(flat, w_hidden, preferred_element_type=jnp.float32)).astype(
        jnp.bfloat16
    )
    pre = jnp.dot(hidden, w_feature, preferred_element_type=jnp.float32)
    scale = lax.rsqrt(jnp.mean(pre * pre, axis=-1, keepdims=True) + epsilon)
    result = (pre * scale * feat_gain).astype(jnp.bfloat16)
    return result.reshape(section_pixels.shape[:-1] + (w_feature.shape[1],))


def flow_field(feature, ref_rows, offsets):
    rows = feature.shape[-3]
    cols = feature.shape[-2]
    padding = [(0, 0)] * (ref_rows.ndim - 2) + [(2, 2), (0, 0)]
    padded = jnp.pad(ref_rows, padding)
    own = feature.astype(jnp.float32)
    scores = {}
    for shift_y in range(-2, 3):
        for shift_x in range(-2, 3):
            window = padded[
                ..., 2 + shift_y : 2 + shift_y + rows, 2 + shift_x : 2 + shift_x + cols, :
            ]
            scores[shift_y, shift_x] = (
                jnp.sum(own * window.astype(jnp.float32), axis=-1) / own.shape[-1]
            )
    offset_y = offsets[..., 0, :, :]
    offset_x = offsets[..., 1, :, :]
    total = jnp.ones(offset_y.shape, jnp.float32)
    sum_y = jnp.zeros(offset_y.shape, jnp.float32)
    sum_x = jnp.zeros(offset_y.shape, jnp.float32)
    for near_y in (-1, 0, 1):
        for near_x in (-1, 0, 1):
            picked = jnp.zeros(offset_y.shape, jnp.float32)
            for cand_y in (-1, 0, 1):
                for cand_x in (-1, 0, 1):
                    hit = (offset_y == cand_y) & (offset_x == cand_x)
                    picked = picked + jnp.where(hit, scores[cand_y + near_y, cand_x + near_x], 0.0)
            weight = picked * picked
            total = total + weight
            sum_y = sum_y + weight * near_y
            sum_x = sum_x + weight * near_x
    flow_y = offset_y.astype(jnp.float32) + sum_y / total
    flow_x = offset_x.astype(jnp.float32) + sum_x / total
    return jnp.stack([flow_y, flow_x], axis=-3)


def relax_step(padded, flow, weight):
    center = padded[:, :, 1:-1]
    upper = padded[:, :, :-2]
    lower = padded[:, :, 2:]
    sided = jnp.pad(center, ((0, 0), (0, 0), (0, 0), (1, 1)))
    left_side = sided[..., :-2]
    right_side = sided[..., 2:]
    return center + step_size * (
        upper + lower + left_side + right_side - 4.0 * center + weight * (flow - center)
    )


def add_fields(earlier, later):
    return earlier + later


def grid_rows(rows, depth):
    global_row = (
        lax.axis_index("tile") * rows + jnp.arange(rows + 2 * depth, dtype=jnp.int32) - depth
    )
    return ((global_row >= 0) & (global_row < rows * lax.axis_size("tile"))).astype(jnp.float32)


def shards(pixels, pred_features, offsets, valid_mask, base_shift, w_hidden, w_feature, feat_gain):
    features = encode(pixels, w_hidden, w_feature, feat_gain)
    is_first = lax.axis_index("sec") == 0
    passed = from_behind(features[-1], "sec", 1)
    first_ref = jnp.where(is_first, pred_features, passed)
    ref_stack = jnp.concatenate([first_ref[None], features[:-1]], axis=0)
    extended = with_halo(ref_stack, (("tile", 1),), 2)
    flow = flow_field(features, extended, offsets)
    weight = stiffness * valid_mask.astype(jnp.float32)[:, None]
    field = jnp.zeros(flow.shape, jnp.float32)
    rows = field.shape[2]
    targets = with_halo(
        jnp.concatenate([flow, weight], axis=1).astype(jnp.bfloat16), (("tile", 2),), ITERS
    ).astype(jnp.float32)
    inside = grid_rows(rows, ITERS)
    field = jnp.zeros(
        (field.shape[0], field.shape[1], rows + 2 * ITERS, field.shape[3]), jnp.float32
    )
    for step in range(ITERS):
        start = step + 1
        length = rows + 2 * ITERS - 2 * start
        flow_part = targets[:, :2, start : start + length]
        weight_part = targets[:, 2:, start : start + length]
        field = (
            relax_step(field, flow_part, weight_part)
            * inside[start : start + length][None, None, :, None]
        )
    local_total = jnp.sum(field, axis=0)
    prefix = entering(local_total, "sec", add_fields, jnp.zeros_like(local_total))
    running = base_shift + prefix
    results = []
    for index in range(field.shape[0]):
        running = running + field[index]
        results.append(running)
    return jnp.stack(results, axis=0)


def solution(mesh):
    in_specs = (
        P("sec", "tile", None, None),
        P("tile", None, None),
        P("sec", None, "tile", None),
        P("sec", "tile", None),
        P(None, "tile", None),
        P(),
        P(),
        P(),
    )
    out_specs = P("sec", None, "tile", None)
    return jax.shard_map(shards, mesh=mesh, in_specs=in_specs, out_specs=out_specs, check_vma=False)
```

profile of v0, /device:TPU:4, one launch (start us, length us, event | category | flops | bytes accessed | tf_op | source)
XLA Modules:
  0.0 199.8 jit_solution(6425203859313015886)
XLA Ops:
  0.0 0.9 copy-done
  1.0 13.5 %multiply_reduce_fusion.24 = (f32[16384]{0:T(1024)S(1)}, f32[16384,128]{1,0:T(8,128)}) fusion(bf16[512,128]{1,0:T(8,128)(2,1)} %param.16, bf16[16384,256]{1,0:T(8,128)(2,1)} %bitcast.951, bf16[256,512]{1,0:T(8,128)(2,1)S(1)} %copy-done), kind=kOutput, calls=%fused_computation.32 | convolution fusion | flops 6463406080 | bytes 17235968 | tf_op jit(solution)/shard_map/dot_general | solution.py:55
  14.5 5.3 %multiply_convert_fusion = bf16[16384,128]{1,0:T(8,128)(2,1)S(1)} fusion(f32[16384,128]{1,0:T(8,128)} %get-tuple-element.106, f32[128]{0:T(128)S(1)} %copy-done.11, f32[16384]{0:T(1024)S(1)} %add_rsqrt_fusion), kind=kLoop, calls=%fused_computation.31 | loop fusion | flops 6291456 | bytes 12648960 | tf_op jit(solution)/shard_map/convert_element_type | solution.py:57
  19.8 1.9 copy-done.4
  21.8 1.7 fusion.196
  23.4 4.8 %collective-permute-start = (bf16[8,1024,128]{2,1,0:T(8,128)(2,1)S(1)}, bf16[8,1024,128]{2,1,0:T(8,128)(2,1)}, u32[]{:S(2)}, u32[]{:S(2)}) collective-permute-start(bf16[8,1024,128]{2,1,0:T(8,128)(2,1)S(1)} %bitcast.949), channel_id=1, source_target_pairs={{0,1},{1,2},{2,3},{4,5},{5,6},{6,7},{8,9},{9,10},{10,11},{12,13},{... | collective-permute-start | bytes 6291464 | tf_op jit(solution)/shard_map/ppermute | solution.py:17
  28.2 0.6 slice.390
  28.8 0.6 slice.342
  29.4 0.7 slice.350
  30.1 0.5 slice.358
  30.6 0.6 slice.366
  31.3 0.6 slice.374
  31.9 0.6 slice.382
  32.5 0.6 slice_multiply_fusion.1
  33.3 0.6 fusion.197
  33.9 37.8 %collective-permute-done = bf16[8,1024,128]{2,1,0:T(8,128)(2,1)} collective-permute-done((bf16[8,1024,128]{2,1,0:T(8,128)(2,1)S(1)}, bf16[8,1024,128]{2,1,0:T(8,128)(2,1)}, u32[]{:S(2)}, u32[]{:S(2)}) %collective-permute-start) | collective-permute-done | bytes 2097184 | tf_op jit(solution)/shard_map/ppermute | solution.py:17
  71.8 2.0 select_bitcast_fusion
  74.2 1.5 fusion.6
  75.6 2.0 %collective-permute-start.2 = (bf16[2,2,1024,128]{3,2,1,0:T(8,128)(2,1)}, bf16[2,2,1024,128]{3,2,1,0:T(8,128)(2,1)S(1)}, u32[]{:S(2)}, u32[]{:S(2)}) collective-permute-start(bf16[2,2,1024,128]{3,2,1,0:T(8,128)(2,1)} %get-tuple-element.92), channel_id=1, source_target_pairs={{4,0},{8,4},{12,8},{16,12},{20,16},{24,20},{28,24},{5,1},{9,5},{13... | collective-permute-start | bytes 3145736 | tf_op jit(solution)/shard_map/ppermute | solution.py:30
  77.7 2.6 %collective-permute-start.1 = (bf16[2,2,1024,128]{3,2,1,0:T(8,128)(2,1)}, bf16[2,2,1024,128]{3,2,1,0:T(8,128)(2,1)}, u32[]{:S(2)}, u32[]{:S(2)}) collective-permute-start(bf16[2,2,1024,128]{3,2,1,0:T(8,128)(2,1)} %get-tuple-element.91), channel_id=1, source_target_pairs={{0,4},{4,8},{8,12},{12,16},{16,20},{20,24},{24,28},{1,5},{5,9},{9,... | collective-permute-start | bytes 3145736 | tf_op jit(solution)/shard_map/ppermute | solution.py:28
  80.3 5.2 %fusion.1 = f32[16384]{0:T(1024)S(1)} fusion(bf16[2,8,1024,128]{3,2,1,0:T(8,128)(2,1)S(1)} %pad_maximum_fusion, f32[128]{0:T(128)S(1)} %copy-done.11, f32[16384,128]{1,0:T(8,128)S(1)} %bitcast.948, f32[16384]{0:T(1024)S(1)} %add_rsqrt_fusion), kind=kLoop, calls=%fused_computation.6 | loop fusion | flops 14663680 | bytes 12714496 | tf_op jit(solution)/shard_map/reduce_sum | solution.py:74
  85.5 13.2 %collective-permute-done.2 = bf16[2,2,1024,128]{3,2,1,0:T(8,128)(2,1)S(1)} collective-permute-done((bf16[2,2,1024,128]{3,2,1,0:T(8,128)(2,1)}, bf16[2,2,1024,128]{3,2,1,0:T(8,128)(2,1)S(1)}, u32[]{:S(2)}, u32[]{:S(2)}) %collective-permute-start.2) | collective-permute-done | bytes 1048608 | tf_op jit(solution)/shard_map/ppermute | solution.py:30
  98.7 4.7 %collective-permute-done.1 = bf16[2,2,1024,128]{3,2,1,0:T(8,128)(2,1)} collective-permute-done((bf16[2,2,1024,128]{3,2,1,0:T(8,128)(2,1)}, bf16[2,2,1024,128]{3,2,1,0:T(8,128)(2,1)}, u32[]{:S(2)}, u32[]{:S(2)}) %collective-permute-start.1) | collective-permute-done | bytes 1048608 | tf_op jit(solution)/shard_map/ppermute | solution.py:28
  103.4 4.8 %select_maximum_fusion = bf16[2,12,1028,128]{3,2,1,0:T(8,128)(2,1)S(1)} fusion(bf16[2,2,1024,128]{3,2,1,0:T(8,128)(2,1)S(1)} %collective-permute-done.2, bf16[2,2,1024,128]{3,2,1,0:T(8,128)(2,1)} %collective-permute-done.1, bf16[1,8,1024,128]{3,2,1,0:T(8,128)(2,1)} %bitcast.942, bf16[1,8,1024,128]{3,2,1,0:T(8,128)(2,1)S(1)} %select_bitcast_fusion), kind=kLoop, calls=%fused_computation.34 | loop fusion | flops 47370240 | bytes 12607488 | tf_op jit(solution)/shard_map/concatenate | solution.py:26
  108.2 4.6 %maximum_maximum_fusion = (bf16[2,10,1024,128]{3,2,1,0:T(8,128)(2,1)S(1)}, bf16[2,10,1024,128]{3,2,1,0:T(8,128)(2,1)}) fusion(bf16[1,8,1024,128]{3,2,1,0:T(8,128)(2,1)S(1)} %bitcast.945, bf16[1,8,1024,128]{3,2,1,0:T(8,128)(2,1)S(1)} %select_bitcast_fusion, bf16[2,2,1024,128]{3,2,1,0:T(8,128)(2,1)} %collective-permute-done.1, ...), kind=kLoop, calls=%fused_computation.44 | loop fusion | flops 10485760 | bytes 16777216 | tf_op jit(solution)/shard_map/concatenate | solution.py:26
  112.8 16.6 %multiply_reduce_fusion.20 = (f32[2,8,1024]{2,1,0:T(8,128)S(1)}, f32[2,8,1024]{2,1,0:T(8,128)S(1)}, f32[2,8,1024]{2,1,0:T(8,128)S(1)}, f32[2,8,1024]{2,1,0:T(8,1...) fusion(bf16[2,12,1028,128]{3,2,1,0:T(8,128)(2,1)S(1)} %select_maximum_fusion, ...), kind=kLoop, calls=%fused_computation.27 | loop fusion | flops 39747584 | bytes 38141952 | tf_op jit(solution)/shard_map/reduce_sum | solution.py:74
  129.4 43.2 %multiply_reduce_fusion.23 = (f32[2,8,1024]{2,1,0:T(8,128)S(1)}, f32[2,8,1024]{2,1,0:T(8,128)S(1)}, f32[2,8,1024]{2,1,0:T(8,128)S(1)}, f32[2,8,1024]{2,1,0:T(8,1...) fusion(f32[2,8,1024,128]{3,2,1,0:T(8,128)} %get-tuple-element.7, ...), kind=kLoop, calls=%fused_computation.30 | loop fusion | flops 112951296 | bytes 85065728 | tf_op jit(solution)/shard_map/reduce_sum | solution.py:74
  173.3 1.9 collective-permute-start.4
  175.2 2.6 %collective-permute-start.3 = (bf16[2,3,8,1024]{3,2,1,0:T(8,128)(2,1)S(1)}, bf16[2,3,8,1024]{3,2,1,0:T(8,128)(2,1)S(1)}, u32[]{:S(2)}, u32[]{:S(2)}) collective-permute-start(bf16[2,3,8,1024]{3,2,1,0:T(8,128)(2,1)S(1)} %pad_maximum_fusion.3), channel_id=1, source_target_pairs={{0,4},{4,8},{8,12},{12,16},{16,20},{20,24},{24,28},{1,5},{5,9},{9,... | collective-permute-start | bytes 294920 | tf_op jit(solution)/shard_map/ppermute | solution.py:28
  177.9 4.1 %collective-permute-done.3 = bf16[2,3,8,1024]{3,2,1,0:T(8,128)(2,1)S(1)} collective-permute-done((bf16[2,3,8,1024]{3,2,1,0:T(8,128)(2,1)S(1)}, bf16[2,3,8,1024]{3,2,1,0:T(8,128)(2,1)S(1)}, u32[]{:S(2)}, u32[]{:S(2)}) %collective-permute-start.3) | collective-permute-done | bytes 98336 | tf_op jit(solution)/shard_map/ppermute | solution.py:28
  184.5 14.6 %all-gather = bf16[8,8,1024]{2,1,0:T(8,128)(2,1)S(1)} all-gather(bf16[2,8,1024]{2,1,0:T(8,128)(2,1)S(1)} %get-tuple-element.65), channel_id=2, replica_groups=mesh['tile'=8,'sec'=4] {'sec'}, dimensions={0}, use_global_device_ids=true | all-gather | bytes 163840 | tf_op jit(solution)/shard_map/all_gather | solution.py:39
  199.2 0.6 copy-done.21
  (89 shorter events, 3.5 us)
Async XLA Ops:
  0.0 1.0 copy-start
  1.0 13.6 %copy-start.11 = (f32[128]{0:T(128)S(1)}, f32[128]{0:T(128)}, u32[]{:S(2)}) copy-start(f32[128]{0:T(128)} %param.17) | copy-start | bytes 1540
  14.5 18.6 %copy-start.9 = (s32[2,8,1024]{2,1,0:T(8,128)S(1)}, s32[2,8,1024]{2,1,0:T(8,128)}, u32[]{:S(2)}) copy-start(s32[2,8,1024]{2,1,0:T(8,128)} %param.13) | copy-start | bytes 196612
  14.5 18.6 %copy-start.6 = (s32[2,2,8,1024]{3,2,1,0:T(8,128)S(1)}, s32[2,2,8,1024]{3,2,1,0:T(8,128)}, u32[]{:S(2)}) copy-start(s32[2,2,8,1024]{3,2,1,0:T(8,128)} %param.12) | copy-start | bytes 393220
  19.8 1.9 copy-start.4
  23.4 48.3 %collective-permute-start = (bf16[8,1024,128]{2,1,0:T(8,128)(2,1)S(1)}, bf16[8,1024,128]{2,1,0:T(8,128)(2,1)}, u32[]{:S(2)}, u32[]{:S(2)}) collective-permute-start(bf16[8,1024,128]{2,1,0:T(8,128)(2,1)S(1)} %bitcast.949), channel_id=1, source_target_pairs={{0,1},{1,2},{2,3},{4,5},{5,6},{6,7},{8,9},{9,10},{10,11},{12,13},{... | collective-permute-start | bytes 6291464 | tf_op jit(solution)/shard_map/ppermute | solution.py:17
  32.5 41.2 %copy-start.2 = (bf16[8192,128]{1,0:T(8,128)(2,1)S(1)}, bf16[8192,128]{1,0:T(8,128)(2,1)}, u32[]{:S(2)}) copy-start(bf16[8192,128]{1,0:T(8,128)(2,1)} %get-tuple-element.94) | copy-start | bytes 6291460
  71.8 8.5 %slice-start = ((s8[8388608]{0:T(1024)(128)(4,1)}), s8[4194304]{0:T(1024)(128)(4,1)S(1)}, s32[]{:S(2)}) async-start(s8[8388608]{0:T(1024)(128)(4,1)} %bitcast.947), calls=%async_computation | async-start | bytes 8388608
  73.8 6.5 %slice-start.1 = ((s8[8388608]{0:T(1024)(128)(4,1)}), s8[4194304]{0:T(1024)(128)(4,1)S(1)}, s32[]{:S(2)}) async-start(s8[8388608]{0:T(1024)(128)(4,1)} %bitcast.947), calls=%async_computation.1 | async-start | bytes 8388608
  75.6 23.1 %collective-permute-start.2 = (bf16[2,2,1024,128]{3,2,1,0:T(8,128)(2,1)}, bf16[2,2,1024,128]{3,2,1,0:T(8,128)(2,1)S(1)}, u32[]{:S(2)}, u32[]{:S(2)}) collective-permute-start(bf16[2,2,1024,128]{3,2,1,0:T(8,128)(2,1)} %get-tuple-element.92), channel_id=1, source_target_pairs={{4,0},{8,4},{12,8},{16,12},{20,16},{24,20},{28,24},{5,1},{9,5},{13... | collective-permute-start | bytes 3145736 | tf_op jit(solution)/shard_map/ppermute | solution.py:30
  77.7 25.7 %collective-permute-start.1 = (bf16[2,2,1024,128]{3,2,1,0:T(8,128)(2,1)}, bf16[2,2,1024,128]{3,2,1,0:T(8,128)(2,1)}, u32[]{:S(2)}, u32[]{:S(2)}) collective-permute-start(bf16[2,2,1024,128]{3,2,1,0:T(8,128)(2,1)} %get-tuple-element.91), channel_id=1, source_target_pairs={{0,4},{4,8},{8,12},{12,16},{16,20},{20,24},{24,28},{1,5},{5,9},{9,... | collective-permute-start | bytes 3145736 | tf_op jit(solution)/shard_map/ppermute | solution.py:28
  85.5 22.7 %copy-start.3 = (bf16[8192,128]{1,0:T(8,128)(2,1)S(1)}, bf16[8192,128]{1,0:T(8,128)(2,1)}, u32[]{:S(2)}) copy-start(bf16[8192,128]{1,0:T(8,128)(2,1)} %get-tuple-element.94) | copy-start | bytes 6291460
  108.2 4.6 %copy-start.5 = (bf16[16384,128]{1,0:T(8,128)(2,1)S(1)}, bf16[16384,128]{1,0:T(8,128)(2,1)}, u32[]{:S(2)}) copy-start(bf16[16384,128]{1,0:T(8,128)(2,1)} %copy-done.4) | copy-start | bytes 12582916
  129.4 43.2 %copy-start.7 = (pred[2,1,8,1024]{3,2,0,1:T(8,128)(4,1)S(1)}, pred[2,1,8,1024]{3,2,0,1:T(8,128)(4,1)}, u32[]{:S(2)}) copy-start(pred[2,1,8,1024]{3,2,0,1:T(8,128)(4,1)} %get-tuple-element.103) | copy-start | bytes 49156
  129.4 43.2 %copy-start.8 = (pred[2,1,8,1024]{3,2,0,1:T(8,128)(4,1)S(1)}, pred[2,1,8,1024]{3,2,0,1:T(8,128)(4,1)}, u32[]{:S(2)}) copy-start(pred[2,1,8,1024]{3,2,0,1:T(8,128)(4,1)} %get-tuple-element.104) | copy-start | bytes 49156
  129.4 52.9 %copy-start.12 = (f32[22]{0:T(128)S(1)}, f32[22]{0:T(128)}, u32[]{:S(2)}) copy-start(f32[22]{0:T(128)} %slice_multiply_fusion.1) | copy-start | bytes 268
  172.5 9.9 %copy-start.19 = (f32[20]{0:T(128)S(1)}, f32[20]{0:T(128)}, u32[]{:S(2)}) copy-start(f32[20]{0:T(128)} %slice.342) | copy-start | bytes 244
  172.5 10.3 %copy-start.18 = (f32[18]{0:T(128)S(1)}, f32[18]{0:T(128)}, u32[]{:S(2)}) copy-start(f32[18]{0:T(128)} %slice.350) | copy-start | bytes 220
  172.6 10.7 %copy-start.17 = (f32[16]{0:T(128)S(1)}, f32[16]{0:T(128)}, u32[]{:S(2)}) copy-start(f32[16]{0:T(128)} %slice.358) | copy-start | bytes 196
  172.6 10.9 %copy-start.16 = (f32[14]{0:T(128)S(1)}, f32[14]{0:T(128)}, u32[]{:S(2)}) copy-start(f32[14]{0:T(128)} %slice.366) | copy-start | bytes 172
  172.6 11.2 %copy-start.15 = (f32[12]{0:T(128)S(1)}, f32[12]{0:T(128)}, u32[]{:S(2)}) copy-start(f32[12]{0:T(128)} %slice.374) | copy-start | bytes 148
  173.2 10.8 %copy-start.14 = (f32[10]{0:T(128)S(1)}, f32[10]{0:T(128)}, u32[]{:S(2)}) copy-start(f32[10]{0:T(128)} %slice.382) | copy-start | bytes 124
  173.3 4.6 %collective-permute-start.4 = (bf16[2,3,8,1024]{3,2,1,0:T(8,128)(2,1)S(1)}, bf16[2,3,8,1024]{3,2,1,0:T(8,128)(2,1)S(1)}, u32[]{:S(2)}, u32[]{:S(2)}) collective-permute-start(bf16[2,3,8,1024]{3,2,1,0:T(8,128)(2,1)S(1)} %pad_maximum_fusion.3), channel_id=1, source_target_pairs={{4,0},{8,4},{12,8},{16,12},{20,16},{24,20},{28,24},{5,1},{9,5},{13... | collective-permute-start | bytes 294920 | tf_op jit(solution)/shard_map/ppermute | solution.py:30
  175.2 6.8 %collective-permute-start.3 = (bf16[2,3,8,1024]{3,2,1,0:T(8,128)(2,1)S(1)}, bf16[2,3,8,1024]{3,2,1,0:T(8,128)(2,1)S(1)}, u32[]{:S(2)}, u32[]{:S(2)}) collective-permute-start(bf16[2,3,8,1024]{3,2,1,0:T(8,128)(2,1)S(1)} %pad_maximum_fusion.3), channel_id=1, source_target_pairs={{0,4},{4,8},{8,12},{12,16},{16,20},{20,24},{24,28},{1,5},{5,9},{9,... | collective-permute-start | bytes 294920 | tf_op jit(solution)/shard_map/ppermute | solution.py:28
  182.1 2.2 %copy-start.13 = (f32[8]{0:T(128)S(1)}, f32[8]{0:T(128)}, u32[]{:S(2)}) copy-start(f32[8]{0:T(128)} %slice.390) | copy-start | bytes 100
  182.3 16.8 %copy-start.10 = (f32[2,8,1024]{2,1,0:T(8,128)S(1)}, f32[2,8,1024]{2,1,0:T(8,128)}, u32[]{:S(2)}) copy-start(f32[2,8,1024]{2,1,0:T(8,128)} %param.14) | copy-start | bytes 196612
  182.3 16.8 %copy-start.20 = (f32[2,2,8,1024]{3,2,1,0:T(8,128)S(1)}, f32[2,2,8,1024]{3,2,1,0:T(8,128)}, u32[]{:S(2)}) copy-start(f32[2,2,8,1024]{3,2,1,0:T(8,128)} %custom-call) | copy-start | bytes 393220
  182.3 17.5 %copy-start.1 = (bf16[256,512]{1,0:T(8,128)(2,1)S(1)}, bf16[256,512]{1,0:T(8,128)(2,1)}, u32[]{:S(2)}) copy-start(bf16[256,512]{1,0:T(8,128)(2,1)} %param.15) | copy-start | bytes 786436
  199.1 0.7 copy-start.21
where the time goes:
time: 200 us
  other arithmetic  87.3 us (44%)
  waiting for transfers between devices  59.8 us (30%)
  blocking collectives  14.6 us (7%)
  starting transfers between devices  13.9 us (7%)
  matrix products  13.5 us (7%)
  local copies, waits for them, and re-layouts  9.92 us (5%)
    reduce_sum x3, other arithmetic, flow_field(): jnp.sum(own * window.astype(jnp.float32), axis=-1) / own.shape[-1]  64.9 us
    ppermute x1, waiting for transfers between devices, from_behind(): lax.ppermute(value, axis, [(source, source + steps) for source in range(f...  37.8 us
    all_gather x1, blocking collectives, entering(): lax.all_gather(value.astype(jnp.bfloat16 if value.dtype == jnp.float32 el...  14.6 us
    dot_general x1, matrix products, encode(): pre = jnp.dot(hidden, w_feature, preferred_element_type=jnp.float32)  13.5 us
    ppermute x2, waiting for transfers between devices, with_halo(): lax.ppermute(head, axis, [((i + 1) % count, i) for i in range(ends)])  13.2 us
    concatenate x2, other arithmetic, with_halo(): jnp.concatenate([lax.ppermute(tail, axis, [(i, (i + 1) % count) for i in...  9.31 us
    ppermute x2, waiting for transfers between devices, with_halo(): lax.ppermute(tail, axis, [(i, (i + 1) % count) for i in range(ends)])  8.83 us
    convert_element_type x1, other arithmetic, encode(): result = (pre * scale * feat_gain).astype(jnp.bfloat16)  5.28 us
  transfers between devices with their start and end apart: 5, of which 4 were waited for; matrix products, arithmetic and copies ran while one was open for 5% of the time, Pallas kernels for 0%

commit v1 on v0

v1 whole, which is shorter than its diff:
```python
import functools

import jax
import jax.numpy as jnp
from jax import lax
from jax.experimental import pallas as pl
from jax.experimental.pallas import tpu as pltpu
from jax.sharding import PartitionSpec as P

ITERS = 8
REACH = 2
LANES = 128
BASE = 16
PAD = LANES
SEG = 16
EDGE = 16

epsilon = 1e-05
step_size = 0.2
stiffness = 0.5

F32 = jnp.float32
BF16 = jnp.bfloat16
HBM = pl.BlockSpec(memory_space=pl.ANY)
VMEM = pl.BlockSpec(memory_space=pltpu.VMEM)
UNROLL = 8


def hop(value, axis, steps):
    count = lax.axis_size(axis)
    pairs = [(i, i + steps) for i in range(count) if 0 <= i + steps < count]
    return lax.ppermute(value, axis, pairs)


def hop_plane(value, steps):
    tiles = lax.axis_size("tile")
    secs = lax.axis_size("sec")
    pairs = [(i * secs, (i + steps) * secs) for i in range(tiles) if 0 <= i + steps < tiles]
    return lax.ppermute(value, ("tile", "sec"), pairs)


def params(limit=48):
    return pltpu.CompilerParams(vmem_limit_bytes=limit * 1024 * 1024)


def encode_chunk(pix, wh, wf, gain):
    hidden = jnp.maximum(jnp.dot(pix, wh, preferred_element_type=F32), 0.0).astype(BF16)
    pre = jnp.dot(hidden, wf, preferred_element_type=F32)
    mean = jnp.mean(pre * pre, axis=-1, keepdims=True)
    return (pre * lax.rsqrt(mean + epsilon) * gain).astype(BF16)


def chunk_of(width):
    for parts in (2, 3, 4):
        if width % (parts * 16) == 0 and width // parts <= 264:
            return width // parts
    return width


def encode_groups(groups, pix_ref, wh_ref, wf_ref, gain_ref, pix_s, sem):
    copies = []
    at = 0
    for sec, row0, nrows, col0, width, _, _ in groups:
        copy = pltpu.make_async_copy(
            pix_ref.at[sec, row0 : row0 + nrows, col0 : col0 + width, :],
            pix_s.at[at : at + nrows, 0:width, :],
            sem.at[len(copies)],
        )
        copy.start()
        copies.append(copy)
        at += nrows
    at = 0
    for copy, (_, _, nrows, _, width, store, done) in zip(copies, groups):
        copy.wait()
        chunk = chunk_of(width)
        parts = width // chunk

        def body(n, carry, at=at, parts=parts, chunk=chunk, store=store):
            row = n // parts
            offset = pl.multiple_of((n % parts) * chunk, 16)
            value = encode_chunk(
                pix_s[at + row, pl.ds(offset, chunk), :], wh_ref[...], wf_ref[...], gain_ref[...]
            )
            store(row, offset, chunk, value)
            return carry

        lax.fori_loop(0, nrows * parts, body, 0)
        done()
        at += nrows


def store_rows(ref, first):
    def store(row, offset, chunk, value):
        ref[first + row, pl.ds(offset, chunk), :] = value

    return store


def nothing():
    pass


def encode_edge_kernel(half, pix_ref, wh_ref, wf_ref, gain_ref, fwd_ref, pix_s, sem):
    width = fwd_ref.shape[1]
    rows = pix_ref.shape[1]
    groups = [
        (1, 0, REACH, 0, width, store_rows(fwd_ref, 0), nothing),
        (1, rows - REACH, REACH, 0, width, store_rows(fwd_ref, REACH), nothing),
    ]
    encode_groups(groups, pix_ref, wh_ref, wf_ref, gain_ref, pix_s, sem)


def encode_cross_kernel(
    half, pix_ref, wh_ref, wf_ref, gain_ref, off_ref, mask_ref, fwd_ref, bwd_ref, pix_s, sem
):
    width = fwd_ref.shape[1]
    rows, cols = pix_ref.shape[1:3]

    def store_bwd(row, offset, chunk, value):
        at = pl.multiple_of(row * width + offset, 16)
        bwd_ref[pl.ds(at, chunk), :] = value

    groups = [
        (0, 0, rows, cols - width, width, store_bwd, nothing),
        (1, REACH, rows - 2 * REACH, 0, width, store_rows(fwd_ref, 0), nothing),
    ]
    first = half // LANES - 1
    for tile in range(cols // LANES - first):
        lanes = slice((first + tile) * LANES, (first + tile + 1) * LANES)
        extra = jnp.concatenate(
            [off_ref[0, 0, :, lanes], off_ref[0, 1, :, lanes], mask_ref[0, :, lanes], mask_ref[0, :, lanes]], 0
        )
        at = rows * width + tile * 4 * rows
        bwd_ref[at : at + 4 * rows, :] = extra.astype(F32).astype(BF16)
    encode_groups(groups, pix_ref, wh_ref, wf_ref, gain_ref, pix_s, sem)


def encode_border_kernel(
    half, pix_ref, wh_ref, wf_ref, gain_ref, edge_ref, bwd_ref,
    eb_ref, ob_ref, up_ref, down_ref, pix_s, sem, csem,
):
    rows, cols = pix_ref.shape[1:3]
    width = edge_ref.shape[1]
    rest = cols - half
    copies = []

    def copy(src, dst):
        c = pltpu.make_async_copy(src, dst, csem.at[len(copies)])
        c.start()
        copies.append(c)

    for pack, row0, edge0 in ((up_ref, rows - REACH, REACH), (down_ref, 0, 0)):
        for r in range(REACH):
            copy(
                bwd_ref.at[pl.ds((row0 + r) * width + width - rest, rest), :],
                pack.at[r, half : half + rest, :],
            )
            copy(
                edge_ref.at[edge0 + r, half - 2 * EDGE : half, :],
                pack.at[r, cols : cols + 2 * EDGE, :],
            )

    def store_both(ref, first, pack, lead):
        def store(row, offset, chunk, value):
            ref[first + row, pl.ds(offset, chunk), :] = value
            pack[row, pl.ds(pl.multiple_of(lead + offset, 16), chunk), :] = value

        return store

    groups = []
    for pack, row0, first in ((down_ref, 0, 0), (up_ref, rows - REACH, REACH)):
        groups.append((0, row0, REACH, 0, half, store_both(eb_ref, first, pack, 0), nothing))
        groups.append(
            (1, row0, REACH, half, rest, store_both(ob_ref, first, pack, cols + 2 * EDGE), nothing)
        )
    encode_groups(groups, pix_ref, wh_ref, wf_ref, gain_ref, pix_s, sem)
    for c in copies:
        c.wait()


def encode_inner_kernel(half, pix_ref, wh_ref, wf_ref, gain_ref, ei_ref, oi_ref, pix_s, sem):
    rows, cols = pix_ref.shape[1:3]
    inner = rows - 2 * REACH
    groups = [
        (0, REACH, inner, 0, half, store_rows(ei_ref, 0), nothing),
        (1, REACH, inner, half, cols - half, store_rows(oi_ref, 0), nothing),
    ]
    encode_groups(groups, pix_ref, wh_ref, wf_ref, gain_ref, pix_s, sem)


def flops_of(nodes, patch, hid, feat):
    return pl.CostEstimate(
        flops=2 * nodes * hid * (patch + feat), bytes_accessed=nodes * 2 * (patch + feat), transcendentals=nodes
    )


def align(band, first, row, lane):
    band = pltpu.roll(band, (2 * LANES - first - BASE + 2) % LANES, 1)
    for shift in (1, 2, 4):
        band = jnp.where((row & shift) != 0, pltpu.roll(band, LANES - shift, 1), band)
    return band


def score_tile(q_s, ref_s, s_s, r, k, low):
    lane = lax.broadcasted_iota(jnp.int32, (8, LANES), 1)
    row = lax.broadcasted_iota(jnp.int32, (8, LANES), 0)
    span = 2 * REACH + 1
    query = q_s[r, pl.ds(pl.multiple_of(k * LANES + low, 16), LANES - low), :]
    products = []
    for a in range(span):
        start = pl.multiple_of(k * LANES + (PAD - BASE - SEG * a), 16)
        window = ref_s[r + a, pl.ds(start, 2 * LANES), :]
        products.append(
            lax.dot_general(query, window, (((1,), (1,)), ((), ())), preferred_element_type=F32)
        )
    groups = [jnp.zeros((8, LANES), F32)] * (low // 8)
    for i in range(low // 8, LANES // 8):
        at = 8 * i - low
        pieces = []
        for a in range(span):
            s = 8 * i + BASE - 4 + SEG * a
            if s < LANES:
                pieces.append((s, a, 0))
            if s + SEG > LANES:
                pieces.append((max(s, LANES) - LANES, a, LANES))
        band = None
        for s, a, h in sorted(pieces):
            value = products[a][at : at + 8, h : h + LANES]
            band = value if band is None else jnp.where(lane >= s, value, band)
        groups.append(align(band, 8 * i, row, lane))
    turned = jnp.concatenate(groups, 0).T
    s_s[r, :, pl.ds(pl.multiple_of(k * LANES, LANES), LANES)] = turned[: SEG * span]


def score_job(q_s, ref_s, s_s, tiles, low=0):
    rows = q_s.shape[0]
    first = 1 if low else 0
    count = tiles - first

    def body(n, carry):
        score_tile(q_s, ref_s, s_s, n // count, n % count + first, 0)
        return carry

    lax.fori_loop(0, rows * count, body, 0, unroll=UNROLL)
    if low:

        def edge(r, carry):
            score_tile(q_s, ref_s, s_s, r, 0, low)
            return carry

        lax.fori_loop(0, rows, edge, 0, unroll=4)


def flow_tile(s_s, oy, ox, lanes):
    y_low, y_high, x_low, x_high = oy < 0, oy > 0, ox < 0, ox > 0
    feat = F32(1.0 / LANES)
    by_row = {}
    for i in range(3):
        for b in range(5):
            v = [s_s[:, SEG * (i + d) + b, lanes] for d in range(3)]
            by_row[i, b] = jnp.where(y_low, v[0], jnp.where(y_high, v[2], v[1]))
    total = jnp.ones_like(oy)
    sum_y = jnp.zeros_like(oy)
    sum_x = jnp.zeros_like(oy)
    for i in range(3):
        for j in range(3):
            near = jnp.where(
                x_low, by_row[i, j], jnp.where(x_high, by_row[i, j + 2], by_row[i, j + 1])
            )
            near = near * feat
            weight = near * near
            total = total + weight
            if i != 1:
                sum_y = sum_y + weight * (i - 1)
            if j != 1:
                sum_x = sum_x + weight * (j - 1)
    return oy + sum_y / total, ox + sum_x / total


def flows_of(s_s, off_ref, flow_ref, tiles):
    def body(k, carry):
        lanes = pl.ds(pl.multiple_of(k * LANES, LANES), LANES)
        fy, fx = flow_tile(s_s, off_ref[0, :, lanes].astype(F32), off_ref[1, :, lanes].astype(F32), lanes)
        flow_ref[0, :, lanes] = fy
        flow_ref[1, :, lanes] = fx
        return carry

    lax.fori_loop(0, tiles, body, 0)


class Loads:
    def __init__(self, sem, first=0):
        self.sem, self.next, self.open = sem, first, []

    def __call__(self, src, dst):
        copy = pltpu.make_async_copy(src, dst, self.sem.at[self.next])
        copy.start()
        self.next += 1
        self.open.append(copy)

    def wait(self):
        for copy in self.open:
            copy.wait()
        self.open = []


def zero_sides(ref_s, cols):
    side = jnp.zeros((ref_s.shape[0], EDGE, ref_s.shape[2]), BF16)
    ref_s[:, PAD - EDGE : PAD, :] = side
    ref_s[:, PAD + cols : PAD + cols + EDGE, :] = side


def own_scores_kernel(
    half, edge_ref, fwdb_ref, bwd_ref, eb_ref, ei_ref, ob_ref, oi_ref, up_ref, down_ref,
    pred_ref, pup_ref, pdown_ref, off_ref, flow_ref, flow0_ref,
    q_s, ref_s, s_s, q0_s, ref0_s, sem,
):
    rows, cols = q_s.shape[:2]
    width = edge_ref.shape[1]
    rest = cols - half
    last = rows - REACH
    is_first = lax.axis_index("sec") == 0
    base0 = half - LANES
    loads = Loads(sem)
    own = slice(PAD, PAD + half)
    far = slice(PAD + half, PAD + cols)
    for row0, part in ((0, 0), (last, REACH)):
        dst = slice(row0, row0 + REACH)
        ref_dst = slice(row0 + REACH, row0 + 2 * REACH)
        src = slice(part, part + REACH)
        loads(edge_ref.at[src, 0:half, :], q_s.at[dst, 0:half, :])
        loads(ob_ref.at[src], q_s.at[dst, half:cols, :])
        loads(eb_ref.at[src], ref_s.at[ref_dst, own, :])
    loads(fwdb_ref.at[:, 0:half, :], q_s.at[REACH:last, 0:half, :])
    loads(oi_ref, q_s.at[REACH:last, half:cols, :])
    loads(ei_ref, ref_s.at[2 * REACH : rows, own, :])
    for r in range(rows):
        loads(bwd_ref.at[pl.ds(r * width + width - rest, rest), :], ref_s.at[r + REACH, far, :])
    loads(up_ref.at[:, 0:cols, :], ref_s.at[0:REACH, PAD : PAD + cols, :])
    loads(down_ref.at[:, 0:cols, :], ref_s.at[rows + REACH : rows + 2 * REACH, PAD : PAD + cols, :])
    zero_sides(ref_s, cols)
    at = loads.next

    def first_loads():
        loads0 = Loads(sem, at)
        for r in range(rows):
            loads0(
                bwd_ref.at[pl.ds(r * width, width), :],
                q0_s.at[r, LANES + rest - width : LANES + rest, :],
            )
        span = slice(base0, cols)
        to = slice(PAD, PAD + cols - base0)
        loads0(pred_ref.at[:, span, :], ref0_s.at[REACH : rows + REACH, to, :])
        loads0(pup_ref.at[:, span, :], ref0_s.at[0:REACH, to, :])
        loads0(pdown_ref.at[:, span, :], ref0_s.at[rows + REACH : rows + 2 * REACH, to, :])
        return loads0

    @pl.when(is_first)
    def _():
        first_loads().wait()

    loads.wait()
    score_job(q_s, ref_s, s_s, cols // LANES)
    flows_of(s_s, off_ref.at[1], flow_ref, cols // LANES)
    flow0_ref[...] = jnp.zeros_like(flow0_ref)

    @pl.when(is_first)
    def _():
        zero_sides(ref0_s, cols - base0)
        tiles = (cols - base0) // LANES
        score_job(q0_s, ref0_s, s_s, tiles, LANES - EDGE)
        flows_of(s_s, off_ref.at[0, :, :, base0:cols], flow0_ref, tiles)


def back_scores_kernel(
    half, q_ref, edge_ref, fwdb_ref, ob_ref, oi_ref, up_ref, down_ref, flow_ref,
    q_s, ref_s, s_s, off_s, sem,
):
    rows, span = q_s.shape[:2]
    width = edge_ref.shape[1]
    rest = span - LANES
    cols = half + rest
    last = rows - REACH
    loads = Loads(sem)
    for r in range(rows):
        loads(q_ref.at[pl.ds(r * width, width), :], q_s.at[r, span - width : span, :])
    lead = PAD + LANES
    gap = 2 * EDGE
    for row0, part in ((0, 0), (last, REACH)):
        dst = slice(row0 + REACH, row0 + 2 * REACH)
        src = slice(part, part + REACH)
        loads(edge_ref.at[src, half - gap : half, :], ref_s.at[dst, lead - gap : lead, :])
        loads(ob_ref.at[src], ref_s.at[dst, lead : lead + rest, :])
    loads(fwdb_ref.at[:, half - gap : half, :], ref_s.at[2 * REACH : rows, lead - gap : lead, :])
    loads(oi_ref, ref_s.at[2 * REACH : rows, lead : lead + rest, :])
    pack = slice(cols, cols + gap + rest)
    to = slice(lead - gap, lead + rest)
    loads(up_ref.at[:, pack, :], ref_s.at[0:REACH, to, :])
    loads(down_ref.at[:, pack, :], ref_s.at[rows + REACH : rows + 2 * REACH, to, :])
    loads(q_ref.at[rows * width :, :], off_s)
    ref_s[:, lead + rest : lead + rest + EDGE, :] = jnp.zeros((rows + 2 * REACH, EDGE, LANES), BF16)
    loads.wait()
    tiles = span // LANES
    score_job(q_s, ref_s, s_s, tiles, LANES - EDGE)

    def body(k, carry):
        lanes = pl.ds(pl.multiple_of(k * LANES, LANES), LANES)
        extra = off_s[pl.ds(pl.multiple_of(k * 4 * rows, 4 * rows), 4 * rows), :].astype(F32)
        fy, fx = flow_tile(s_s, extra[:rows], extra[rows : 2 * rows], lanes)
        flow_ref[0, :, lanes] = fy
        flow_ref[1, :, lanes] = fx
        flow_ref[2, :, lanes] = extra[2 * rows : 3 * rows]
        return carry

    lax.fori_loop(0, tiles, body, 0)


def pairs_out(pack_ref, at, tops, bottoms):
    for n, (top, bottom) in enumerate(zip(tops, bottoms)):
        pack_ref[at + 16 * n : at + 16 * n + 16, :] = jnp.concatenate([top, bottom], 0).astype(BF16)
    return at + 16 * len(tops)


def front_scores_kernel(
    half, edge_ref, fwdb_ref, up_ref, down_ref, pred_ref, pup_ref, pdown_ref, eb_ref, ei_ref,
    off_ref, mask_ref, flow1_ref, flow0_ref, flow2_ref, flow_ref, pack_ref,
    q_s, ref_s, s_s, sem,
):
    rows = q_s.shape[0]
    cols = off_ref.shape[3]
    width = edge_ref.shape[1]
    last = rows - REACH
    is_first = lax.axis_index("sec") == 0
    loads = Loads(sem)
    for row0, part in ((0, 0), (last, REACH)):
        loads(eb_ref.at[part : part + REACH], q_s.at[row0 : row0 + REACH, :, :])
    loads(ei_ref, q_s.at[REACH:last, :, :])
    at = loads.next
    span = slice(PAD, PAD + width)

    @pl.when(is_first)
    def _():
        mine = Loads(sem, at)
        mine(pred_ref.at[:, 0:width, :], ref_s.at[REACH : rows + REACH, span, :])
        mine(pup_ref.at[:, 0:width, :], ref_s.at[0:REACH, span, :])
        mine(pdown_ref.at[:, 0:width, :], ref_s.at[rows + REACH : rows + 2 * REACH, span, :])
        mine.wait()

    @pl.when(jnp.logical_not(is_first))
    def _():
        mine = Loads(sem, at)
        mine(edge_ref.at[0:REACH], ref_s.at[REACH : 2 * REACH, span, :])
        mine(edge_ref.at[REACH : 2 * REACH], ref_s.at[rows : rows + REACH, span, :])
        mine(fwdb_ref, ref_s.at[2 * REACH : rows, span, :])
        mine(up_ref, ref_s.at[0:REACH, span, :])
        mine(down_ref, ref_s.at[rows + REACH : rows + 2 * REACH, span, :])
        mine.wait()

    loads.wait()
    ref_s[:, PAD - EDGE : PAD, :] = jnp.zeros((rows + 2 * REACH, EDGE, LANES), BF16)
    tiles = half // LANES
    score_job(q_s, ref_s, s_s, tiles)
    flow_ref[:, :, half:cols] = flow0_ref[:, :, LANES:]
    flows_of(s_s, off_ref.at[0], flow_ref, tiles)

    def tiles_of(ref, count):
        return [ref[:, n * LANES : (n + 1) * LANES] for n in range(count)]

    n = 0
    for ref, count in ((flow1_ref, cols // LANES), (flow_ref, cols // LANES), (flow2_ref, flow2_ref.shape[2] // LANES)):
        n = pairs_out(pack_ref, n, tiles_of(ref.at[0], count), tiles_of(ref.at[1], count))
    masks = []
    for ref, count in ((mask_ref.at[1], cols // LANES), (mask_ref.at[0], cols // LANES), (flow2_ref.at[2], flow2_ref.shape[2] // LANES)):
        masks += [m.astype(F32) for m in tiles_of(ref, count)]
    if len(masks) % 2:
        masks.append(masks[-1])
    pairs_out(pack_ref, n, masks[0::2], masks[1::2])


def relax_kernel(
    half, up_ref, down_ref, flow1_ref, flow3_ref, flow2_ref, mask_ref, f1_ref, f3_ref, msg_ref,
    field_s, pull_s, keep_s,
):
    rows, cols = flow1_ref.shape[1:]
    deep = rows + 2 * ITERS
    place = lax.axis_index("tile")
    count = lax.axis_size("tile")
    glob = place * rows + lax.broadcasted_iota(jnp.int32, (deep, LANES), 0) - ITERS
    inside = ((glob >= 0) & (glob < rows * count)).astype(F32)
    widths = (cols, cols, flow2_ref.shape[2])
    tiles = [w // LANES for w in widths]
    flows = (flow1_ref, flow3_ref, flow2_ref)
    own_masks = (mask_ref.at[1], mask_ref.at[0], flow2_ref.at[2])
    starts = [0, tiles[0], tiles[0] + tiles[1]]
    mask_at = 16 * sum(tiles)
    for job in range(3):
        for k in range(tiles[job]):
            lanes = slice(k * LANES, (k + 1) * LANES)
            at = 16 * (starts[job] + k)
            m_at = mask_at + 8 * (starts[job] + k)
            half_at = m_at // 16 * 16
            sub = slice(m_at - half_at, m_at - half_at + 8)
            upper = up_ref[at : at + 16, :].astype(F32)
            lower = down_ref[at : at + 16, :].astype(F32)
            m_up = up_ref[half_at : half_at + 16, :].astype(F32)[sub]
            m_down = down_ref[half_at : half_at + 16, :].astype(F32)[sub]
            weight = stiffness * jnp.concatenate(
                [m_up, own_masks[job][:, lanes].astype(F32), m_down], 0
            )
            keep_s[job, :, lanes] = (step_size - step_size * weight) * inside
            for c in range(2):
                flow = jnp.concatenate(
                    [upper[8 * c : 8 * c + 8], flows[job][c, :, lanes], lower[8 * c : 8 * c + 8]], 0
                )
                pull = step_size * weight * flow * inside
                pull_s[job, c, :, lanes] = pull
                field_s[job, c, :, lanes] = pull
    step = step_size * inside

    def body(n, carry):
        for job in range(3):
            wide = widths[job]
            for c in range(2):
                old = [field_s[job, c, :, k * LANES : (k + 1) * LANES] for k in range(tiles[job])]
                lane = lax.broadcasted_iota(jnp.int32, (deep, LANES), 1)
                nxt = [pltpu.roll(x, LANES - 1, 1) for x in old]
                prv = [pltpu.roll(x, 1, 1) for x in old]
                zero = jnp.zeros_like(old[0])
                for k in range(tiles[job]):
                    lanes = slice(k * LANES, (k + 1) * LANES)
                    right = jnp.where(lane == LANES - 1, nxt[k + 1] if k + 1 < tiles[job] else zero, nxt[k])
                    left = jnp.where(lane == 0, prv[k - 1] if k else zero, prv[k])
                    around = pltpu.roll(old[k], 1, 0) + pltpu.roll(old[k], deep - 1, 0) + left + right
                    field_s[job, c, :, lanes] = (
                        keep_s[job, :, lanes] * old[k] + step * around + pull_s[job, c, :, lanes]
                    )
        return carry

    lax.fori_loop(0, ITERS - 1, body, 0)
    is_first = lax.axis_index("sec") == 0
    seam = half - EDGE // 2
    mine = slice(ITERS, ITERS + rows)
    lead = half - LANES
    for c in range(2):
        for k in range(tiles[0]):
            lanes = slice(k * LANES, (k + 1) * LANES)
            col = lax.broadcasted_iota(jnp.int32, (rows, LANES), 1) + k * LANES
            one = field_s[0, c, mine, lanes]
            front = field_s[1, c, mine, lanes]
            if (k + 1) * LANES > seam:
                front = jnp.where((col < seam) | is_first, front, 0.0)
            total = one + front
            if k * LANES >= lead:
                back = field_s[2, c, mine, k * LANES - lead : (k + 1) * LANES - lead]
                total = total + jnp.where(col >= seam, back, 0.0)
            f1_ref[c, :, lanes] = one
            f3_ref[c, :, lanes] = front
            msg_ref[c, :, lanes] = total.astype(msg_ref.dtype)


def shards(pixels, pred, offsets, mask, base_shift, w_hidden, w_feature, feat_gain):
    secs, rows, cols, patch = pixels.shape
    hid, feat = w_feature.shape
    assert secs == 2 and rows == ITERS and feat == LANES and cols % (2 * LANES) == 0
    half = cols // 2
    rest = cols - half
    width = half + EDGE
    inner = rows - 2 * REACH
    span = rest + LANES
    deep = rows + 2 * REACH
    tail = 4 * rows * (span // LANES)
    gain = feat_gain.reshape(1, feat)
    shape = jax.ShapeDtypeStruct
    weights = (w_hidden, w_feature, gain)
    is_first = lax.axis_index("sec") == 0

    pup = hop_plane(pred[rows - REACH :], 1)
    pdown = hop_plane(pred[:REACH], -1)

    edge = pl.pallas_call(
        functools.partial(encode_edge_kernel, half),
        out_shape=shape((2 * REACH, width, feat), BF16),
        in_specs=[HBM, VMEM, VMEM, VMEM],
        out_specs=VMEM,
        scratch_shapes=[pltpu.VMEM((2 * REACH, width, patch), BF16), pltpu.SemaphoreType.DMA((2,))],
        compiler_params=params(),
        cost_estimate=flops_of(2 * REACH * width, patch, hid, feat),
        name="encode_edge",
    )(pixels, *weights)
    edge_in = hop(edge, "sec", 1)

    fwdb, bwd = pl.pallas_call(
        functools.partial(encode_cross_kernel, half),
        out_shape=(shape((inner, width, feat), BF16), shape((rows * width + tail, feat), BF16)),
        in_specs=[HBM, VMEM, VMEM, VMEM, VMEM, VMEM],
        out_specs=(VMEM, VMEM),
        scratch_shapes=[pltpu.VMEM((rows + inner, width, patch), BF16), pltpu.SemaphoreType.DMA((2,))],
        compiler_params=params(),
        cost_estimate=flops_of((rows + inner) * width, patch, hid, feat),
        name="encode_cross",
    )(pixels, *weights, offsets, mask)
    fwdb_in = hop(fwdb, "sec", 1)
    bwd_in = hop(bwd, "sec", -1)

    pack_cols = cols + 2 * EDGE + rest
    eb, ob, up, down = pl.pallas_call(
        functools.partial(encode_border_kernel, half),
        out_shape=(
            shape((2 * REACH, half, feat), BF16),
            shape((2 * REACH, rest, feat), BF16),
            shape((REACH, pack_cols, feat), BF16),
            shape((REACH, pack_cols, feat), BF16),
        ),
        in_specs=[HBM, VMEM, VMEM, VMEM, HBM, HBM],
        out_specs=(VMEM,) * 4,
        scratch_shapes=[
            pltpu.VMEM((4 * REACH, max(half, rest), patch), BF16),
            pltpu.SemaphoreType.DMA((4,)),
            pltpu.SemaphoreType.DMA((4 * REACH,)),
        ],
        compiler_params=params(),
        cost_estimate=flops_of(2 * REACH * cols, patch, hid, feat),
        name="encode_border",
    )(pixels, *weights, edge, bwd)
    up_in = hop(up, "tile", 1)
    down_in = hop(down, "tile", -1)

    ei, oi = pl.pallas_call(
        functools.partial(encode_inner_kernel, half),
        out_shape=(shape((inner, half, feat), BF16), shape((inner, rest, feat), BF16)),
        in_specs=[HBM, VMEM, VMEM, VMEM],
        out_specs=(VMEM, VMEM),
        scratch_shapes=[pltpu.VMEM((2 * inner, max(half, rest), patch), BF16), pltpu.SemaphoreType.DMA((2,))],
        compiler_params=params(),
        cost_estimate=flops_of(inner * cols, patch, hid, feat),
        name="encode_inner",
    )(pixels, *weights)

    fup_in = hop(edge_in[REACH:], "tile", 1)
    fdown_in = hop(edge_in[:REACH], "tile", -1)

    bands = SEG * (2 * REACH + 1)
    nodes = rows * cols

    def score_cost(part):
        return pl.CostEstimate(flops=int(part * nodes * 12 * 2 * 256 * 128), bytes_accessed=int(part * nodes * 512), transcendentals=0)

    flow1, flow0 = pl.pallas_call(
        functools.partial(own_scores_kernel, half),
        out_shape=(shape((2, rows, cols), F32), shape((2, rows, span), F32)),
        in_specs=[HBM] * 12 + [VMEM],
        out_specs=(VMEM, VMEM),
        scratch_shapes=[
            pltpu.VMEM((rows, cols, feat), BF16),
            pltpu.VMEM((deep, cols + 2 * PAD, feat), BF16),
            pltpu.VMEM((rows, bands, cols), F32),
            pltpu.VMEM((rows, span, feat), BF16),
            pltpu.VMEM((deep, span + 2 * PAD, feat), BF16),
            pltpu.SemaphoreType.DMA((32,)),
        ],
        compiler_params=params(),
        cost_estimate=score_cost(1.0),
        name="own_scores",
    )(edge, fwdb, bwd, eb, ei, ob, oi, up_in, down_in, pred, pup, pdown, offsets)

    flow2 = pl.pallas_call(
        functools.partial(back_scores_kernel, half),
        out_shape=shape((3, rows, span), F32),
        in_specs=[HBM] * 7,
        out_specs=VMEM,
        scratch_shapes=[
            pltpu.VMEM((rows, span, feat), BF16),
            pltpu.VMEM((deep, span + 2 * PAD, feat), BF16),
            pltpu.VMEM((rows, bands, span), F32),
            pltpu.VMEM((tail, feat), BF16),
            pltpu.SemaphoreType.DMA((20,)),
        ],
        compiler_params=params(),
        cost_estimate=score_cost(0.55),
        name="back_scores",
    )(bwd_in, edge, fwdb, ob, oi, up_in, down_in)

    tiles = 2 * (cols // LANES) + span // LANES
    pack_rows = 16 * tiles + 16 * ((tiles + 1) // 2)
    flow3, pack = pl.pallas_call(
        functools.partial(front_scores_kernel, half),
        out_shape=(shape((2, rows, cols), F32), shape((pack_rows, LANES), BF16)),
        in_specs=[HBM] * 9 + [VMEM] * 5,
        out_specs=(VMEM, VMEM),
        scratch_shapes=[
            pltpu.VMEM((rows, half, feat), BF16),
            pltpu.VMEM((deep, half + 3 * PAD, feat), BF16),
            pltpu.VMEM((rows, bands, half), F32),
            pltpu.SemaphoreType.DMA((12,)),
        ],
        compiler_params=params(),
        cost_estimate=score_cost(0.5),
        name="front_scores",
    )(edge_in, fwdb_in, fup_in, fdown_in, pred, pup, pdown, eb, ei, offsets, mask, flow1, flow0, flow2)
    pack_up = hop(pack, "tile", 1)
    pack_down = hop(pack, "tile", -1)

    wide = 24 if rows == 8 else rows + 2 * ITERS
    f1, f3, msg = pl.pallas_call(
        functools.partial(relax_kernel, half),
        out_shape=(shape((2, rows, cols), F32), shape((2, rows, cols), F32), shape((2, rows, cols), BF16)),
        in_specs=[VMEM] * 6,
        out_specs=(VMEM,) * 3,
        scratch_shapes=[
            pltpu.VMEM((3, 2, wide, cols), F32),
            pltpu.VMEM((3, 2, wide, cols), F32),
            pltpu.VMEM((3, wide, cols), F32),
        ],
        compiler_params=params(),
        cost_estimate=pl.CostEstimate(flops=nodes * 24 * 12 * 8, bytes_accessed=nodes * 40, transcendentals=0),
        name="relax",
    )(pack_up, pack_down, flow1, flow3, flow2, mask)

    prefix = base_shift
    for steps in range(1, lax.axis_size("sec")):
        prefix = prefix + hop(msg, "sec", steps).astype(F32)
    first = prefix + f3
    return jnp.stack([first, first + f1], axis=0)


def solution(mesh):
    in_specs = (
        P("sec", "tile", None, None),
        P("tile", None, None),
        P("sec", None, "tile", None),
        P("sec", "tile", None),
        P(None, "tile", None),
        P(),
        P(),
        P(),
    )
    out_specs = P("sec", None, "tile", None)
    return jax.shard_map(shards, mesh=mesh, in_specs=in_specs, out_specs=out_specs, check_vma=False)
```

time: 200 us -> 137 us (0.69)
  other arithmetic: 87.3 us -> 0.69 us
  Pallas kernels: 0 us -> 83.6 us
  waiting for transfers between devices: 59.8 us -> 15.1 us
  starting transfers between devices: 13.9 us -> 33.7 us
  blocking collectives: 14.6 us -> 0 us
  matrix products: 13.5 us -> 0 us
  local copies, waits for them, and re-layouts: 9.92 us -> 2.64 us
    pallas_call x0 -> x8, Pallas kernels: none -> 83.6 us  [the longest x1 22.7 us: shards(): pl.pallas_call(functools.partial(own_scores_kernel, half), out_shape=(sha...]
    reduce_sum x4 -> x0, other arithmetic: 65.1 us -> none  [the longest x3 64.9 us: flow_field(): jnp.sum(own * window.astype(jnp.float32), axis=-1) / own.shape[-1]]
    ppermute x5 -> x14, waiting for transfers between devices: 59.8 us -> 15.1 us  [the longest x2 8.57 us: hop_plane(): return lax.ppermute(value, ('tile', 'sec'), pairs)]
    ppermute x5 -> x14, starting transfers between devices: 13.9 us -> 33.7 us  [the longest x12 27.2 us: hop(): return lax.ppermute(value, axis, pairs)]
    all_gather x1 -> x0, blocking collectives: 14.6 us -> none  [entering(): lax.all_gather(value.astype(jnp.bfloat16 if value.dtype == jnp.float32 el...]
    dot_general x1 -> x0, matrix products: 13.5 us -> none  [encode(): pre = jnp.dot(hidden, w_feature, preferred_element_type=jnp.float32)]
    concatenate x5 -> x0, other arithmetic: 11.2 us -> none  [the longest x2 9.31 us: with_halo(): jnp.concatenate([lax.ppermute(tail, axis, [(i, (i + 1) % count) for i in...]
    slice x16 -> x2, local copies, waits for them, and re-layouts: 6.15 us -> 0.11 us  [the longest x1 0.07 us: shards(): pdown = hop_plane(pred[:REACH], -1)]
  transfers between devices with their start and end apart: 5 -> 14, of which waited for: 4 -> 5; matrix products, arithmetic and copies ran while one was open for 5% -> 0% of each run, Pallas kernels for 0% -> 49%
where the time goes in v1:
time: 137 us; the launch traced here: 136 us
  Pallas kernels  83.6 us (61%)
  starting transfers between devices  33.7 us (25%)
  waiting for transfers between devices  15.1 us (11%)
  local copies, waits for them, and re-layouts  2.64 us (2%)
    ppermute x12, starting transfers between devices, hop(): return lax.ppermute(value, axis, pairs)  27.2 us
    pallas_call x1, Pallas kernels, shards(): pl.pallas_call(functools.partial(own_scores_kernel, half), out_shape=(sha...  22.7 us
    pallas_call x1, Pallas kernels, shards(): pl.pallas_call(functools.partial(encode_cross_kernel, half), out_shape=(s...  16.9 us
    pallas_call x1, Pallas kernels, shards(): pl.pallas_call(functools.partial(back_scores_kernel, half), out_shape=sha...  9.83 us
    pallas_call x1, Pallas kernels, shards(): pl.pallas_call(functools.partial(encode_border_kernel, half), out_shape=(...  9.43 us
    ppermute x2, waiting for transfers between devices, hop_plane(): return lax.ppermute(value, ('tile', 'sec'), pairs)  8.57 us
    pallas_call x1, Pallas kernels, shards(): pl.pallas_call(functools.partial(encode_inner_kernel, half), out_shape=(s...  8.48 us
    pallas_call x1, Pallas kernels, shards(): pl.pallas_call(functools.partial(front_scores_kernel, half), out_shape=(s...  7.47 us
  transfers between devices with their start and end apart: 14, of which 5 were waited for; matrix products, arithmetic and copies ran while one was open for 0% of the time, Pallas kernels for 49%

profile of v1, /device:TPU:4, one launch (start us, length us, event | category | flops | bytes accessed | tf_op | source)
XLA Modules:
  0.0 136.1 jit_solution(14066471762071383077)
XLA Ops:
  0.0 0.9 copy-done
  1.0 0.9 copy-done.1
  1.9 0.7 copy-done.4
  2.5 6.2 %encode_edge.1.edge_ref = bf16[4,528,128]{2,1,0:T(8,128)(2,1)S(1)} custom-call(bf16[2,8,1024,256]{3,2,1,0:T(8,128)(2,1)} %pix_ref.7, bf16[256,512]{1,0:T(8,128)(2,1)S(1)} %copy-done, bf16[512,128]{1,0:T(8,128)(2,1)S(1)} %copy-done.1, f32[1,128]{1,0:T(1,128)S(1)} %bitcast.4), custom_call_target="tpu_custom_call" | custom-call | flops 830472192 | bytes 1622016 | tf_op jit(solution)/shard_map/encode_edge/pallas_call | solution.py:580
  8.7 3.5 %collective-permute-start = (bf16[4,528,128]{2,1,0:T(8,128)(2,1)S(1)}, bf16[4,528,128]{2,1,0:T(8,128)(2,1)S(1)}, u32[]{:S(2)}, u32[]{:S(2)}) collective-permute-start(bf16[4,528,128]{2,1,0:T(8,128)(2,1)S(1)} %encode_edge.1.edge_ref), channel_id=1, source_target_pairs={{0,1},{1,2},{2,3},{4,5},{5,6},{6,7},{8,9},{9,10},{10,11},{12,13},{... | collective-permute-start | bytes 1622024 | tf_op jit(solution)/shard_map/ppermute | solution.py:32
  12.3 16.9 %encode_cross.1 = (bf16[4,528,128]{2,1,0:T(8,128)(2,1)S(1)}, bf16[4384,128]{1,0:T(8,128)(2,1)S(1)}) custom-call(bf16[2,8,1024,256]{3,2,1,0:T(8,128)(2,1)} %pix_ref.7, bf16[256,512]{1,0:T(8,128)(2,1)S(1)} %copy-done, bf16[512,128]{1,0:T(8,128)(2,1)S(1)} %copy-done.1, f32[1,128]{1,0:T(1,128)S(1)} %bitcast.5, s32[2,2,8,1024]{3,2,1,0:T(8,128)S(1)} %copy-done.6, ...), custom_call_target="tpu_custom_call" | custom-call | flops 2491416576 | bytes 4866048 | tf_op jit(solution)/shard_map/encode_cross/pallas_call | solution.py:592
  29.2 9.4 %encode_border.1 = (bf16[4,512,128]{2,1,0:T(8,128)(2,1)S(1)}, bf16[4,512,128]{2,1,0:T(8,128)(2,1)S(1)}, bf16[2,1568,128]{2,1,0:T(8,128)(2,1)S(1)}, bf16[2,1568,128]{2,1,0:T(8,128)(2,1)S(1)}) custom-call(bf16[2,8,1024,256]{3,2,1,0:T(8,128)(2,1)} %pix_ref.7, bf16[256,512]{1,0:T(8,128)(2,1)S(1)} %copy-done, bf16[512,128]{1,0:T(8,128)(2,1)S(1)} %copy-done.1, ...), custom_call_target="tpu_custom_call" | custom-call | flops 1610612736 | bytes 3145728 | tf_op jit(solution)/shard_map/encode_border/pallas_call | solution.py:606
  38.7 1.9 %collective-permute-start.6 = (bf16[2,1568,128]{2,1,0:T(8,128)(2,1)S(1)}, bf16[2,1568,128]{2,1,0:T(8,128)(2,1)S(1)}, u32[]{:S(2)}, u32[]{:S(2)}) collective-permute-start(bf16[2,1568,128]{2,1,0:T(8,128)(2,1)S(1)} %get-tuple-element.26), channel_id=1, source_target_pairs={{0,4},{4,8},{8,12},{12,16},{16,20},{20,24},{24,28},{1,5},{5,9},{9,... | collective-permute-start | bytes 2408456 | tf_op jit(solution)/shard_map/ppermute | solution.py:32
  40.6 4.5 %collective-permute-start.7 = (bf16[2,1568,128]{2,1,0:T(8,128)(2,1)S(1)}, bf16[2,1568,128]{2,1,0:T(8,128)(2,1)S(1)}, u32[]{:S(2)}, u32[]{:S(2)}) collective-permute-start(bf16[2,1568,128]{2,1,0:T(8,128)(2,1)S(1)} %get-tuple-element.27), channel_id=1, source_target_pairs={{4,0},{8,4},{12,8},{16,12},{20,16},{24,20},{28,24},{5,1},{9,5},{13... | collective-permute-start | bytes 2408456 | tf_op jit(solution)/shard_map/ppermute | solution.py:32
  45.2 0.1 fusion
  45.2 1.9 %collective-permute-start.4 = (bf16[2,1024,128]{2,1,0:T(8,128)(2,1)S(1)}, bf16[2,1024,128]{2,1,0:T(8,128)(2,1)S(1)}, u32[]{:S(2)}, u32[]{:S(2)}) collective-permute-start(bf16[2,1024,128]{2,1,0:T(8,128)(2,1)S(1)} %get-tuple-element.38), channel_id=1, source_target_pairs={{0,4},{4,8},{8,12},{12,16},{16,20},{20,24},{24,28}} | collective-permute-start | bytes 1572872 | tf_op jit(solution)/shard_map/ppermute | solution.py:39
  47.2 4.5 %collective-permute-start.5 = (bf16[2,1024,128]{2,1,0:T(8,128)(2,1)S(1)}, bf16[2,1024,128]{2,1,0:T(8,128)(2,1)S(1)}, u32[]{:S(2)}, u32[]{:S(2)}) collective-permute-start(bf16[2,1024,128]{2,1,0:T(8,128)(2,1)S(1)} %get-tuple-element.37), channel_id=1, source_target_pairs={{4,0},{8,4},{12,8},{16,12},{20,16},{24,20},{28,24}} | collective-permute-start | bytes 1572872 | tf_op jit(solution)/shard_map/ppermute | solution.py:39
  51.7 1.3 collective-permute-start.8
  53.0 8.5 %encode_inner.1 = (bf16[4,512,128]{2,1,0:T(8,128)(2,1)S(1)}, bf16[4,512,128]{2,1,0:T(8,128)(2,1)S(1)}) custom-call(bf16[2,8,1024,256]{3,2,1,0:T(8,128)(2,1)} %pix_ref.7, bf16[256,512]{1,0:T(8,128)(2,1)S(1)} %copy-done, bf16[512,128]{1,0:T(8,128)(2,1)S(1)} %copy-done.1, f32[1,128]{1,0:T(1,128)S(1)} %bitcast.7), custom_call_target="tpu_custom_call" | custom-call | flops 1610612736 | bytes 3145728 | tf_op jit(solution)/shard_map/encode_inner/pallas_call | solution.py:628
  61.6 8.6 %collective-permute-done.4.pup_ref = bf16[2,1024,128]{2,1,0:T(8,128)(2,1)S(1)} collective-permute-done((bf16[2,1024,128]{2,1,0:T(8,128)(2,1)S(1)}, bf16[2,1024,128]{2,1,0:T(8,128)(2,1)S(1)}, u32[]{:S(2)}, u32[]{:S(2)}) %collective-permute-start.4) | collective-permute-done | bytes 524320 | tf_op jit(solution)/shard_map/ppermute | solution.py:39
  70.2 1.3 collective-permute-start.1
  71.5 1.9 %collective-permute-start.2 = (bf16[2,528,128]{2,1,0:T(8,128)(2,1)S(1)}, bf16[2,528,128]{2,1,0:T(8,128)(2,1)S(1)}, u32[]{:S(2)}, u32[]{:S(2)}) collective-permute-start(bf16[2,528,128]{2,1,0:T(8,128)(2,1)S(1)} %get-tuple-element.40), channel_id=1, source_target_pairs={{0,4},{4,8},{8,12},{12,16},{16,20},{20,24},{24,28},{1,5},{5,9},{9,... | collective-permute-start | bytes 811016 | tf_op jit(solution)/shard_map/ppermute | solution.py:32
  73.4 4.5 %collective-permute-start.3 = (bf16[2,528,128]{2,1,0:T(8,128)(2,1)S(1)}, bf16[2,528,128]{2,1,0:T(8,128)(2,1)S(1)}, u32[]{:S(2)}, u32[]{:S(2)}) collective-permute-start(bf16[2,528,128]{2,1,0:T(8,128)(2,1)S(1)} %get-tuple-element.39), channel_id=1, source_target_pairs={{4,0},{8,4},{12,8},{16,12},{20,16},{24,20},{28,24},{5,1},{9,5},{13... | collective-permute-start | bytes 811016 | tf_op jit(solution)/shard_map/ppermute | solution.py:32
  78.0 22.7 %own_scores.1 = (f32[2,8,1024]{2,1,0:T(8,128)S(1)}, f32[2,8,640]{2,1,0:T(8,128)S(1)}) custom-call(bf16[4,528,128]{2,1,0:T(8,128)(2,1)S(1)} %encode_edge.1.edge_ref, bf16[4,528,128]{2,1,0:T(8,128)(2,1)S(1)} %get-tuple-element.20.fwdb_ref, bf16[4384,128]{1,0:T(8,128)(2,1)} %copy-done.2, bf16[4,512,128]{2,1,0:T(8,128)(2,1)S(1)} %get-tuple-element.22.eb_ref, ...), custom_call_target="tpu_custom_call" | custom-call | flops 6442450944 | bytes 4194304 | tf_op jit(solution)/shard_map/own_scores/pallas_call | solution.py:648
  100.7 9.8 %back_scores.1.flow2_ref = f32[3,8,640]{2,1,0:T(8,128)S(1)} custom-call(bf16[4384,128]{1,0:T(8,128)(2,1)S(1)} %collective-permute-done.8.q_ref, bf16[4,528,128]{2,1,0:T(8,128)(2,1)S(1)} %encode_edge.1.edge_ref, bf16[4,528,128]{2,1,0:T(8,128)(2,1)S(1)} %get-tuple-element.20.fwdb_ref, bf16[4,512,128]{2,1,0:T(8,128)(2,1)S(1)} %get-tuple-element.24.ob_ref, ...), custom_call_target="tpu_custom_call" | custom-call | flops 3543347968 | bytes 2306867 | tf_op jit(solution)/shard_map/back_scores/pallas_call | solution.py:666
  110.6 7.5 %front_scores.1 = (f32[2,8,1024]{2,1,0:T(8,128)S(1)}, bf16[512,128]{1,0:T(8,128)(2,1)S(1)}) custom-call(bf16[4,528,128]{2,1,0:T(8,128)(2,1)S(1)} %collective-permute-done.edge_ref, bf16[4,528,128]{2,1,0:T(8,128)(2,1)S(1)} %collective-permute-done.1.fwdb_ref, bf16[2,528,128]{2,1,0:T(8,128)(2,1)S(1)} %collective-permute-done.2.up_ref, ...), custom_call_target="tpu_custom_call" | custom-call | flops 3221225472 | bytes 2097152 | tf_op jit(solution)/shard_map/front_scores/pallas_call | solution.py:685
  118.0 2.1 %collective-permute-start.10 = (bf16[512,128]{1,0:T(8,128)(2,1)S(1)}, bf16[512,128]{1,0:T(8,128)(2,1)S(1)}, u32[]{:S(2)}, u32[]{:S(2)}) collective-permute-start(bf16[512,128]{1,0:T(8,128)(2,1)S(1)} %get-tuple-element.30), channel_id=1, source_target_pairs={{4,0},{8,4},{12,8},{16,12},{20,16},{24,20},{28,24},{5,1},{9,5},{13... | collective-permute-start | bytes 393224 | tf_op jit(solution)/shard_map/ppermute | solution.py:32
  120.1 2.2 %collective-permute-start.9 = (bf16[512,128]{1,0:T(8,128)(2,1)S(1)}, bf16[512,128]{1,0:T(8,128)(2,1)S(1)}, u32[]{:S(2)}, u32[]{:S(2)}) collective-permute-start(bf16[512,128]{1,0:T(8,128)(2,1)S(1)} %get-tuple-element.30), channel_id=1, source_target_pairs={{0,4},{4,8},{8,12},{12,16},{16,20},{20,24},{24,28},{1,5},{5,9},{9,... | collective-permute-start | bytes 393224 | tf_op jit(solution)/shard_map/ppermute | solution.py:32
  122.4 0.3 collective-permute-done.10.down_ref
  122.6 4.7 %collective-permute-done.9.up_ref = bf16[512,128]{1,0:T(8,128)(2,1)S(1)} collective-permute-done((bf16[512,128]{1,0:T(8,128)(2,1)S(1)}, bf16[512,128]{1,0:T(8,128)(2,1)S(1)}, u32[]{:S(2)}, u32[]{:S(2)}) %collective-permute-start.9) | collective-permute-done | bytes 131104 | tf_op jit(solution)/shard_map/ppermute | solution.py:32
  127.3 2.6 %relax.1 = (f32[2,8,1024]{2,1,0:T(8,128)S(1)}, f32[2,8,1024]{2,1,0:T(8,128)S(1)}, bf16[2,8,1024]{2,1,0:T(8,128)(2,1)S(1)}) custom-call(bf16[512,128]{1,0:T(8,128)(2,1)S(1)} %collective-permute-done.9.up_ref, bf16[512,128]{1,0:T(8,128)(2,1)S(1)} %collective-permute-done.10.down_ref, f32[2,8,1024]{2,1,0:T(8,128)S(1)} %get-tuple-element.28.flow1_ref, ...), custom_call_target="tpu_custom_call" | custom-call | flops 18874368 | bytes 327680 | tf_op jit(solution)/shard_map/relax/pallas_call | solution.py:704
  129.9 1.3 collective-permute-start.11
  131.2 1.3 collective-permute-start.12
  132.5 1.3 collective-permute-start.13
  133.8 0.3 collective-permute-done.12
  134.1 1.3 collective-permute-done.13
  135.4 0.7 pad_maximum_fusion
  (26 shorter events, 0.1 us)
Async XLA Ops:
  0.0 0.9 copy-start
  1.0 0.9 copy-start.1
  1.9 0.7 copy-start.4
  2.5 9.7 %copy-start.3 = (s32[2,8,1024]{2,1,0:T(8,128)S(1)}, s32[2,8,1024]{2,1,0:T(8,128)}, u32[]{:S(2)}) copy-start(s32[2,8,1024]{2,1,0:T(8,128)} %mask_ref.5) | copy-start | bytes 196612
  2.5 9.8 %copy-start.5 = (f32[128]{0:T(128)S(1)}, f32[128]{0:T(128)}, u32[]{:S(2)}) copy-start(f32[128]{0:T(128)} %param.15) | copy-start | bytes 1540
  2.5 9.8 %copy-start.6 = (s32[2,2,8,1024]{3,2,1,0:T(8,128)S(1)}, s32[2,2,8,1024]{3,2,1,0:T(8,128)}, u32[]{:S(2)}) copy-start(s32[2,2,8,1024]{3,2,1,0:T(8,128)} %off_ref.5) | copy-start | bytes 393220
  8.7 43.0 %collective-permute-start = (bf16[4,528,128]{2,1,0:T(8,128)(2,1)S(1)}, bf16[4,528,128]{2,1,0:T(8,128)(2,1)S(1)}, u32[]{:S(2)}, u32[]{:S(2)}) collective-permute-start(bf16[4,528,128]{2,1,0:T(8,128)(2,1)S(1)} %encode_edge.1.edge_ref), channel_id=1, source_target_pairs={{0,1},{1,2},{2,3},{4,5},{5,6},{6,7},{8,9},{9,10},{10,11},{12,13},{... | collective-permute-start | bytes 1622024 | tf_op jit(solution)/shard_map/ppermute | solution.py:32
  29.2 22.5 %copy-start.2 = (bf16[4384,128]{1,0:T(8,128)(2,1)}, bf16[4384,128]{1,0:T(8,128)(2,1)S(1)}, u32[]{:S(2)}) copy-start(bf16[4384,128]{1,0:T(8,128)(2,1)S(1)} %get-tuple-element.21.bwd_ref) | copy-start | bytes 3366916
  29.2 15.9 %copy-start.7 = (bf16[8,1024,128]{2,1,0:T(8,128)(2,1)S(1)}, bf16[8,1024,128]{2,1,0:T(8,128)(2,1)}, u32[]{:S(2)}) copy-start(bf16[8,1024,128]{2,1,0:T(8,128)(2,1)} %pred_ref.3) | copy-start | bytes 6291460
  38.7 34.7 %collective-permute-start.6 = (bf16[2,1568,128]{2,1,0:T(8,128)(2,1)S(1)}, bf16[2,1568,128]{2,1,0:T(8,128)(2,1)S(1)}, u32[]{:S(2)}, u32[]{:S(2)}) collective-permute-start(bf16[2,1568,128]{2,1,0:T(8,128)(2,1)S(1)} %get-tuple-element.26), channel_id=1, source_target_pairs={{0,4},{4,8},{8,12},{12,16},{16,20},{20,24},{24,28},{1,5},{5,9},{9,... | collective-permute-start | bytes 2408456 | tf_op jit(solution)/shard_map/ppermute | solution.py:32
  40.6 37.4 %collective-permute-start.7 = (bf16[2,1568,128]{2,1,0:T(8,128)(2,1)S(1)}, bf16[2,1568,128]{2,1,0:T(8,128)(2,1)S(1)}, u32[]{:S(2)}, u32[]{:S(2)}) collective-permute-start(bf16[2,1568,128]{2,1,0:T(8,128)(2,1)S(1)} %get-tuple-element.27), channel_id=1, source_target_pairs={{4,0},{8,4},{12,8},{16,12},{20,16},{24,20},{28,24},{5,1},{9,5},{13... | collective-permute-start | bytes 2408456 | tf_op jit(solution)/shard_map/ppermute | solution.py:32
  45.2 24.9 %collective-permute-start.4 = (bf16[2,1024,128]{2,1,0:T(8,128)(2,1)S(1)}, bf16[2,1024,128]{2,1,0:T(8,128)(2,1)S(1)}, u32[]{:S(2)}, u32[]{:S(2)}) collective-permute-start(bf16[2,1024,128]{2,1,0:T(8,128)(2,1)S(1)} %get-tuple-element.38), channel_id=1, source_target_pairs={{0,4},{4,8},{8,12},{12,16},{16,20},{20,24},{24,28}} | collective-permute-start | bytes 1572872 | tf_op jit(solution)/shard_map/ppermute | solution.py:39
  47.2 24.3 %collective-permute-start.5 = (bf16[2,1024,128]{2,1,0:T(8,128)(2,1)S(1)}, bf16[2,1024,128]{2,1,0:T(8,128)(2,1)S(1)}, u32[]{:S(2)}, u32[]{:S(2)}) collective-permute-start(bf16[2,1024,128]{2,1,0:T(8,128)(2,1)S(1)} %get-tuple-element.37), channel_id=1, source_target_pairs={{4,0},{8,4},{12,8},{16,12},{20,16},{24,20},{28,24}} | collective-permute-start | bytes 1572872 | tf_op jit(solution)/shard_map/ppermute | solution.py:39
  51.7 48.9 %collective-permute-start.8 = (bf16[4384,128]{1,0:T(8,128)(2,1)S(1)}, bf16[4384,128]{1,0:T(8,128)(2,1)S(1)}, u32[]{:S(2)}, u32[]{:S(2)}) collective-permute-start(bf16[4384,128]{1,0:T(8,128)(2,1)S(1)} %get-tuple-element.21.bwd_ref), channel_id=1, source_target_pairs={{1,0},{2,1},{3,2},{5,4},{6,5},{7,6},{9,8},{10,9},{11,10},{13,12},{... | collective-permute-start | bytes 3366920 | tf_op jit(solution)/shard_map/ppermute | solution.py:32
  70.2 40.4 %collective-permute-start.1 = (bf16[4,528,128]{2,1,0:T(8,128)(2,1)S(1)}, bf16[4,528,128]{2,1,0:T(8,128)(2,1)S(1)}, u32[]{:S(2)}, u32[]{:S(2)}) collective-permute-start(bf16[4,528,128]{2,1,0:T(8,128)(2,1)S(1)} %get-tuple-element.20.fwdb_ref), channel_id=1, source_target_pairs={{0,1},{1,2},{2,3},{4,5},{5,6},{6,7},{8,9},{9,10},{10,11},{12,13},{... | collective-permute-start | bytes 1622024 | tf_op jit(solution)/shard_map/ppermute | solution.py:32
  71.5 39.0 %collective-permute-start.2 = (bf16[2,528,128]{2,1,0:T(8,128)(2,1)S(1)}, bf16[2,528,128]{2,1,0:T(8,128)(2,1)S(1)}, u32[]{:S(2)}, u32[]{:S(2)}) collective-permute-start(bf16[2,528,128]{2,1,0:T(8,128)(2,1)S(1)} %get-tuple-element.40), channel_id=1, source_target_pairs={{0,4},{4,8},{8,12},{12,16},{16,20},{20,24},{24,28},{1,5},{5,9},{9,... | collective-permute-start | bytes 811016 | tf_op jit(solution)/shard_map/ppermute | solution.py:32
  73.4 37.1 %collective-permute-start.3 = (bf16[2,528,128]{2,1,0:T(8,128)(2,1)S(1)}, bf16[2,528,128]{2,1,0:T(8,128)(2,1)S(1)}, u32[]{:S(2)}, u32[]{:S(2)}) collective-permute-start(bf16[2,528,128]{2,1,0:T(8,128)(2,1)S(1)} %get-tuple-element.39), channel_id=1, source_target_pairs={{4,0},{8,4},{12,8},{16,12},{20,16},{24,20},{28,24},{5,1},{9,5},{13... | collective-permute-start | bytes 811016 | tf_op jit(solution)/shard_map/ppermute | solution.py:32
  110.6 24.9 %copy-start.8 = (f32[2,8,1024]{2,1,0:T(8,128)S(1)}, f32[2,8,1024]{2,1,0:T(8,128)}, u32[]{:S(2)}) copy-start(f32[2,8,1024]{2,1,0:T(8,128)} %param.12) | copy-start | bytes 196612
  118.0 4.6 %collective-permute-start.10 = (bf16[512,128]{1,0:T(8,128)(2,1)S(1)}, bf16[512,128]{1,0:T(8,128)(2,1)S(1)}, u32[]{:S(2)}, u32[]{:S(2)}) collective-permute-start(bf16[512,128]{1,0:T(8,128)(2,1)S(1)} %get-tuple-element.30), channel_id=1, source_target_pairs={{4,0},{8,4},{12,8},{16,12},{20,16},{24,20},{28,24},{5,1},{9,5},{13... | collective-permute-start | bytes 393224 | tf_op jit(solution)/shard_map/ppermute | solution.py:32
  120.1 7.2 %collective-permute-start.9 = (bf16[512,128]{1,0:T(8,128)(2,1)S(1)}, bf16[512,128]{1,0:T(8,128)(2,1)S(1)}, u32[]{:S(2)}, u32[]{:S(2)}) collective-permute-start(bf16[512,128]{1,0:T(8,128)(2,1)S(1)} %get-tuple-element.30), channel_id=1, source_target_pairs={{0,4},{4,8},{8,12},{12,16},{16,20},{20,24},{24,28},{1,5},{5,9},{9,... | collective-permute-start | bytes 393224 | tf_op jit(solution)/shard_map/ppermute | solution.py:32
  129.9 3.9 %collective-permute-start.11 = (bf16[2,8,1024]{2,1,0:T(8,128)(2,1)S(1)}, bf16[2,8,1024]{2,1,0:T(8,128)(2,1)S(1)}, u32[]{:S(2)}, u32[]{:S(2)}) collective-permute-start(bf16[2,8,1024]{2,1,0:T(8,128)(2,1)S(1)} %get-tuple-element.32), channel_id=1, source_target_pairs={{0,1},{1,2},{2,3},{4,5},{5,6},{6,7},{8,9},{9,10},{10,11},{12,13},{... | collective-permute-start | bytes 98312 | tf_op jit(solution)/shard_map/ppermute | solution.py:32
  131.2 2.9 %collective-permute-start.12 = (bf16[2,8,1024]{2,1,0:T(8,128)(2,1)S(1)}, bf16[2,8,1024]{2,1,0:T(8,128)(2,1)S(1)}, u32[]{:S(2)}, u32[]{:S(2)}) collective-permute-start(bf16[2,8,1024]{2,1,0:T(8,128)(2,1)S(1)} %get-tuple-element.32), channel_id=1, source_target_pairs={{0,2},{1,3},{4,6},{5,7},{8,10},{9,11},{12,14},{13,15},{16,18},{17,... | collective-permute-start | bytes 98312 | tf_op jit(solution)/shard_map/ppermute | solution.py:32
  132.5 2.9 %collective-permute-start.13 = (bf16[2,8,1024]{2,1,0:T(8,128)(2,1)S(1)}, bf16[2,8,1024]{2,1,0:T(8,128)(2,1)S(1)}, u32[]{:S(2)}, u32[]{:S(2)}) collective-permute-start(bf16[2,8,1024]{2,1,0:T(8,128)(2,1)S(1)} %get-tuple-element.32), channel_id=1, source_target_pairs={{0,3},{4,7},{8,11},{12,15},{16,19},{20,23},{24,27},{28,31}} | collective-permute-start | bytes 98312 | tf_op jit(solution)/shard_map/ppermute | solution.py:32
